TPU v7x, 32 devices: a whole 2x2x4 slice. The times are simulated.
32 devices in a mesh: hyp: 2 (over y), row: 4 (over z), col: 4 (over x, core).
Axes of the slice: x: 2, y: 2, z: 4, core: 2. Of those that a mesh axis runs over, the one named last changes fastest.
Arguments:
- inverse_tile: float32 [16384, 8192], P(('hyp', 'row'), 'col'), parts along dimension 0, may hold values from -32768 to 262144, as said below
- panels: float32 [2, 2, 8192, 512], P('hyp', None, ('col', 'row')), parts along dimension 0, may hold values from -0.0007324219 to 0.0007324219
- link_panel: float32 [2, 512, 512], P('hyp'), parts along dimension 0, may hold values from -0.09375 to 0.09375
- diag_inverse: float32 [2, 2, 512, 512], P('hyp', None, 'row', 'col'), parts along dimension 0, may hold values from -3 to 3
- ancestor_tiles: int32 [1, 2, 64], replicated, may hold values 0 or 1
Outputs:
- ancestor_block: float32 [2, 2, 8192, 512], P('hyp', None, ('row', 'col')), parts along dimension 0
- diag_block: float32 [2, 2, 512, 512], P('hyp', None, 'row', 'col'), parts along dimension 0
- cross_block: float32 [2, 512, 512], P('hyp', 'row', 'col'), parts along dimension 0
There are 2 independent parts, one for each index of `hyp`. A program takes and returns all parts, laid end to end along the dimension named above; an argument that names none is the same for every part. Nothing has to cross between parts.
Inputs may be any that keep to these rules, and one draw needn't show every extreme that they name: `inverse_tile`: symmetric.
All inputs are finite; a program needn't handle non-finite values.
Results may differ from a plain program's by a relative error of at most 0.000075.
Values sent between devices are 32-bit elements; how exact they have to be, the bound alone decides.
A program may use at most 128 MiB of HBM per device.

v0:
```python
import jax
import jax.numpy as jnp
from jax import lax
from jax.sharding import PartitionSpec as P

TILE = 128


precise = lax.Precision.HIGHEST


def broadcast(block, axis, owner):
    block = jnp.where(lax.axis_index(axis) == owner, block, jnp.zeros_like(block))
    return lax.psum(block, axis)


def tile_product(inverse_tile, panel_block):
    return jnp.einsum("ik,skb->sib", inverse_tile, panel_block, precision=precise)


def own_place(row_id, col_id, row_block, col_block):
    root_index = row_id * row_block // col_block
    offset = jnp.clip(row_id * row_block - col_id * col_block, 0, col_block - row_block)
    return (root_index, offset)


def own_rows(panel_block, root_index, offset, row_block):
    own_piece = lax.dynamic_slice_in_dim(panel_block, offset, row_block, 1)
    return broadcast(own_piece, "col", root_index)


def local(inverse_tile, panels, link_panel, diag_inverse, ancestor_tiles):
    row_id = lax.axis_index("row")
    col_id = lax.axis_index("col")
    rows_axis = lax.axis_size("row")
    row_block = inverse_tile.shape[0]
    col_block = inverse_tile.shape[1]
    local_rows = panels.shape[2]
    diag_height = diag_inverse.shape[2]
    diag_span = diag_inverse.shape[3]
    row_start = (col_id * rows_axis + row_id) * local_rows
    tile_mask = jnp.repeat(ancestor_tiles, TILE, axis=2)
    kept_rows = lax.dynamic_slice_in_dim(tile_mask, row_start, local_rows, 2).astype(jnp.float32)
    masked = panels * kept_rows[..., None]
    first_full = lax.all_gather(masked[:, 0], "row", axis=1, tiled=True)
    first_cols = -lax.psum_scatter(
        tile_product(inverse_tile, first_full), "col", scatter_dimension=2, tiled=True
    )
    second_full = lax.all_gather(masked[:, 1], "row", axis=1, tiled=True)
    col_start = col_id * diag_span
    diag_start = row_id * diag_height
    root_index, offset = own_place(row_id, col_id, row_block, col_block)
    first_own = own_rows(first_full, root_index, offset, row_block)
    second_own = own_rows(second_full, root_index, offset, row_block)
    link_cols = lax.dynamic_slice_in_dim(link_panel, col_start, diag_span, 2)
    shifted = second_full - jnp.einsum("sik,skc->sic", first_full, link_panel, precision=precise)
    second_cols = -lax.psum_scatter(
        tile_product(inverse_tile, shifted), "col", scatter_dimension=2, tiled=True
    )
    first_terms = jnp.einsum("sib,sic->sbc", first_own, first_cols, precision=precise)
    cross_terms = jnp.einsum("sib,sic->sbc", first_own, second_cols, precision=precise)
    first_diag_sum, cross_sum = (
        lax.psum_scatter(first_terms, "row", scatter_dimension=1, tiled=True),
        lax.psum_scatter(cross_terms, "row", scatter_dimension=1, tiled=True),
    )
    diag_first = diag_inverse[:, 0] - first_diag_sum
    given_rows = lax.all_gather(diag_inverse[:, 0], "col", axis=2, tiled=True)
    cross_block = -(
        cross_sum + jnp.einsum("sik,skc->sic", given_rows, link_cols, precision=precise)
    )
    stacked_cols = jnp.stack([first_cols, second_cols], axis=1)
    ancestor_block = lax.all_to_all(stacked_cols, "col", split_axis=2, concat_axis=3, tiled=True)
    link_own = lax.dynamic_slice_in_dim(link_panel, diag_start, diag_height, 1)
    second_diag_terms = jnp.einsum(
        "sib,sic->sbc", second_own, second_cols, precision=precise
    ) + jnp.einsum("skb,skc->sbc", link_own, cross_block, precision=precise)
    second_diag_sum = lax.psum_scatter(second_diag_terms, "row", scatter_dimension=1, tiled=True)
    diag_second = diag_inverse[:, 1] - second_diag_sum
    diag_block = jnp.stack([diag_first, diag_second], axis=1)
    return (ancestor_block, diag_block, cross_block)


def solution(mesh):
    in_specs = (
        P(("hyp", "row"), "col"),
        P("hyp", None, ("col", "row"), None),
        P("hyp", None, None),
        P("hyp", None, "row", "col"),
        P(),
    )
    out_specs = (
        P("hyp", None, ("row", "col"), None),
        P("hyp", None, "row", "col"),
        P("hyp", "row", "col"),
    )
    return jax.shard_map(local, mesh=mesh, in_specs=in_specs, out_specs=out_specs, check_vma=False)
```

profile of v0, /device:TPU:0, one launch (start us, length us, event | category | flops | bytes accessed | tf_op | source)
XLA Modules:
  0.0 505.0 jit_solution(8113400781957419094)
XLA Ops:
  8.2 1.8 broadcast_multiply_fusion
  10.0 1.5 fusion.35
  12.3 82.8 %all-gather.8.cloned.1.call-done = f32[1,1,2048,512]{3,2,1,0:T(8,128)} async-done(((f32[1,1,512,512]{3,2,1,0:T(8,128)}), f32[1,1,2048,512]{3,2,1,0:T(8,128)}) %all-gather.8.cloned.1.call-update) | async-done | bytes 4194320 | tf_op jit(solution)/shard_map/all_gather | solution.py:49
  95.1 4.7 fusion.3
  99.8 76.2 %all-gather.6.cloned.1.call-done = f32[1,1,2048,512]{3,2,1,0:T(8,128)} async-done(((f32[1,1,512,512]{3,2,1,0:T(8,128)}), f32[1,1,2048,512]{3,2,1,0:T(8,128)}) %all-gather.6.cloned.1.call-update) | async-done | bytes 4194320 | tf_op jit(solution)/shard_map/all_gather | solution.py:45
  175.9 4.6 select_bitcast_fusion
  180.6 8.7 %fusion.4 = f32[2048,512]{1,0:T(8,128)S(1)} fusion(f32[1,1,2048,512]{3,2,1,0:T(8,128)} %all-gather.6.cloned.1.call-done, f32[1,512,512]{2,1,0:T(8,128)S(1)} %copy-done), kind=kOutput, calls=%fused_computation.6 | convolution fusion | flops 6442450944 | bytes 9437184 | tf_op jit(solution)/shard_map/sik,skc->sic/dot_general | solution.py:56
  189.3 57.2 %fusion.11 = f32[1,2048,512]{1,2,0:T(8,128)} fusion(f32[2048,2048]{1,0:T(8,128)} %param.5, f32[2048,512]{1,0:T(8,128)S(1)} %fusion.4, f32[1,1,2048,512]{3,2,1,0:T(8,128)S(1)} %copy-done.2), kind=kOutput, calls=%fused_computation.12 | convolution fusion | flops 25770852352 | bytes 29360128 | tf_op jit(solution)/shard_map/ik,skb->sib/dot_general | solution.py:18
  246.6 57.6 %fusion.8 = f32[1,2048,512]{1,2,0:T(8,128)} fusion(f32[2048,2048]{1,0:T(8,128)} %param.5, f32[1,1,2048,512]{3,2,1,0:T(8,128)} %all-gather.6.cloned.1.call-done), kind=kOutput, calls=%fused_computation.11 | convolution fusion | flops 25769803776 | bytes 25165824 | tf_op jit(solution)/shard_map/ik,skb->sib/dot_general | solution.py:18
  305.0 7.3 %all-gather.2 = f32[1,1,128,512]{3,2,1,0:T(8,128)S(1)} all-gather(f32[1,1,128,128]{3,2,1,0:T(8,128)S(1)} %slice-done), channel_id=4, replica_groups=mesh['hyp'=2,'row'=4,'col'=4] {'col'}, dimensions={3}, use_global_device_ids=true | all-gather | bytes 327680 | tf_op jit(solution)/shard_map/all_gather | solution.py:67
  312.3 21.2 %all-reduce.3.cloned.1.call-done = (f32[2048,512]{1,0:T(8,128)}, f32[2048,512]{1,0:T(8,128)}) async-done(((f32[2048,512]{1,0:T(8,128)}, f32[2048,512]{1,0:T(8,128)}), (f32[2048,512]{1,0:T(8,128)}, f32[2048,512]{1,0:T(8,128)})) %all-reduce.3.cloned.1.call-update) | async-done | bytes 8388624 | tf_op jit(solution)/shard_map/psum | solution.py:14
  333.5 47.1 %reduce-scatter.8.cloned.1.call-done = f32[1,2048,128]{1,2,0:T(8,128)} async-done(((f32[1,2048,512]{1,2,0:T(8,128)}), f32[1,2048,128]{1,2,0:T(8,128)}) %reduce-scatter.8.cloned.1.call-update) | async-done | bytes 1048592 | tf_op jit(solution)/shard_map/reduce_scatter | solution.py:57
  380.6 9.9 %convolution_bitcast_fusion = f32[1,512,128]{2,1,0:T(8,128)} fusion(f32[2048,512]{1,0:T(8,128)} %get-tuple-element.4, f32[1,2048,128]{1,2,0:T(8,128)} %reduce-scatter.8.cloned.1.call-done), kind=kOutput, calls=%fused_computation.16 | convolution fusion | flops 1610874880 | bytes 5505024 | tf_op jit(solution)/shard_map/sib,sic->sbc/dot_general | solution.py:61
  390.7 36.9 %reduce-scatter.6.cloned.1.call-done = f32[1,2048,128]{1,2,0:T(8,128)} async-done(((f32[1,2048,512]{1,2,0:T(8,128)}), f32[1,2048,128]{1,2,0:T(8,128)}) %reduce-scatter.6.cloned.1.call-update) | async-done | bytes 1048592 | tf_op jit(solution)/shard_map/reduce_scatter | solution.py:46
  427.6 1.3 negate_bitcast_fusion
  428.9 1.5 pad_maximum_fusion
  430.4 4.2 copy.10
  434.7 4.5 all-to-all-start
  439.5 9.6 %convolution_bitcast_fusion.1 = f32[1,512,128]{2,1,0:T(8,128)} fusion(f32[2048,512]{1,0:T(8,128)} %get-tuple-element.4, f32[1,2048,128]{1,2,0:T(8,128)S(1)} %copy-done.3), kind=kOutput, calls=%fused_computation.17 | convolution fusion | flops 1610874880 | bytes 5505024 | tf_op jit(solution)/shard_map/sib,sic->sbc/dot_general | solution.py:60
  449.4 8.5 %fusion.18 = f32[512,128]{1,0:T(8,128)S(1)} fusion(f32[2048,512]{1,0:T(8,128)} %get-tuple-element.3, f32[1,2048,128]{1,2,0:T(8,128)S(1)} %copy-done.1), kind=kOutput, calls=%fused_computation.22 | convolution fusion | flops 1610874880 | bytes 5505024 | tf_op jit(solution)/shard_map/sib,sic->sbc/dot_general | solution.py:74
  460.5 10.3 %reduce-scatter.10.cloned.1.call-done = f32[1,128,128]{2,1,0:T(8,128)} async-done(((f32[1,512,128]{2,1,0:T(8,128)}), f32[1,128,128]{2,1,0:T(8,128)}) %reduce-scatter.10.cloned.1.call-update) | async-done | bytes 65552 | tf_op jit(solution)/shard_map/reduce_scatter | solution.py:63
  470.8 20.5 %reduce-scatter.14.cloned.1.call-done = f32[1,128,128]{2,1,0:T(8,128)} async-done(((f32[1,512,128]{2,1,0:T(8,128)}), f32[1,128,128]{2,1,0:T(8,128)}) %reduce-scatter.14.cloned.1.call-update) | async-done | bytes 65552 | tf_op jit(solution)/shard_map/reduce_scatter | solution.py:77
  492.9 2.9 copy.11
  495.8 1.8 all_to_all.16
  (40 shorter events, 7.6 us)
Async XLA Ops:
  7.2 173.5 %copy-start = (f32[1,512,512]{2,1,0:T(8,128)S(1)}, f32[1,512,512]{2,1,0:T(8,128)}, u32[]{:S(2)}) copy-start(f32[1,512,512]{2,1,0:T(8,128)} %param.7) | copy-start | bytes 3145732
  7.2 87.9 %all-gather.8.cloned.1.call-start = ((), (), s32[]{:S(2)}) async-start(), calls=%async_computation.12 | async-start | bytes 5242880 | tf_op jit(solution)/shard_map/all_gather | solution.py:49
  11.5 164.4 %all-gather.6.cloned.1.call-start = ((), (), s32[]{:S(2)}) async-start(), calls=%async_computation.11 | async-start | bytes 5242880 | tf_op jit(solution)/shard_map/all_gather | solution.py:45
  12.2 321.3 %all-reduce.3.cloned.1.call-start = ((), (), s32[]{:S(2)}) async-start(), calls=%async_computation.13 | async-start | bytes 16777216 | tf_op jit(solution)/shard_map/psum | solution.py:14
  180.6 200.0 %reduce-scatter.8.cloned.1.call-start = ((), (), s32[]{:S(2)}) async-start(), calls=%async_computation.7 | async-start | bytes 5242880 | tf_op jit(solution)/shard_map/reduce_scatter | solution.py:57
  180.6 8.7 %copy-start.2 = (f32[1,1,2048,512]{3,2,1,0:T(8,128)S(1)}, f32[1,1,2048,512]{3,2,1,0:T(8,128)}, u32[]{:S(2)}) copy-start(f32[1,1,2048,512]{3,2,1,0:T(8,128)} %all-gather.8.cloned.1.call-done) | copy-start | bytes 12582916
  246.6 181.0 %reduce-scatter.6.cloned.1.call-start = ((), (), s32[]{:S(2)}) async-start(), calls=%async_computation.6 | async-start | bytes 5242880 | tf_op jit(solution)/shard_map/reduce_scatter | solution.py:46
  304.2 0.8 slice-start
  304.2 153.7 %reduce-scatter.12.cloned.1.call-start = ((), (), s32[]{:S(2)}) async-start(), calls=%async_computation.9 | async-start | bytes 327680 | tf_op jit(solution)/shard_map/reduce_scatter | solution.py:64
  380.6 10.0 %copy-start.1 = (f32[1,2048,128]{1,2,0:T(8,128)S(1)}, f32[1,2048,128]{1,2,0:T(8,128)}, u32[]{:S(2)}) copy-start(f32[1,2048,128]{1,2,0:T(8,128)} %reduce-scatter.8.cloned.1.call-done) | copy-start | bytes 3145732
  430.4 9.0 %copy-start.3 = (f32[1,2048,128]{1,2,0:T(8,128)S(1)}, f32[1,2048,128]{1,2,0:T(8,128)}, u32[]{:S(2)}) copy-start(f32[1,2048,128]{1,2,0:T(8,128)} %reduce-scatter.6.cloned.1.call-done) | copy-start | bytes 3145732
  434.7 58.2 %all-to-all-start = ((f32[1,2,2048,128]{3,1,0,2:T(2,128)}), f32[1,2,2048,128]{3,1,0,2:T(2,128)}, u32[]{:S(2)}, u32[]{:S(2)}) async-start(f32[1,2,2048,128]{3,1,0,2:T(2,128)} %copy.10), calls=%async_computation.2 | async-start | bytes 4194304 | tf_op jit(solution)/shard_map/all_to_all | solution.py:72
  439.2 31.6 %reduce-scatter.10.cloned.1.call-start = ((), (), s32[]{:S(2)}) async-start(), calls=%async_computation.8 | async-start | bytes 327680 | tf_op jit(solution)/shard_map/reduce_scatter | solution.py:63
  449.0 42.3 %copy-start.4 = (f32[1,2,128,128]{3,2,1,0:T(8,128)S(1)}, f32[1,2,128,128]{3,2,1,0:T(8,128)}, u32[]{:S(2)}) copy-start(f32[1,2,128,128]{3,2,1,0:T(8,128)} %param.8) | copy-start | bytes 393220
  449.1 42.3 %reduce-scatter.14.cloned.1.call-start = ((), (), s32[]{:S(2)}) async-start(), calls=%async_computation.10 | async-start | bytes 327680 | tf_op jit(solution)/shard_map/reduce_scatter | solution.py:77
  459.1 38.5 %copy-start.5 = (f32[1,128,128]{2,1,0:T(8,128)}, f32[1,128,128]{2,1,0:T(8,128)S(1)}, u32[]{:S(2)}) copy-start(f32[1,128,128]{2,1,0:T(8,128)S(1)} %fusion.16) | copy-start | bytes 196612
Sparse Core Ops, SparseCore 0:
  11.6 83.4 all-gather.7
  96.7 79.2 all-gather.5
  180.7 152.7 all-reduce.2
  335.9 44.6 reduce-scatter.7
  383.0 44.5 reduce-scatter.5
  429.7 19.9 reduce-scatter.11
  452.6 18.2 reduce-scatter.9
  473.1 18.2 reduce-scatter.13
where the time goes:
time: 510 us; the launch traced here: 505 us
  waiting for transfers between devices  296 us (58%)
  matrix products  154 us (30%)
  other arithmetic  15.5 us (3%)
  between operations  14.8 us (3%)
  local copies, waits for them, and re-layouts  12.2 us (2%)
  blocking collectives  7.29 us (1%)
  starting transfers between devices  5.38 us (1%)
    dot_general x2, matrix products, tile_product(): jnp.einsum('ik,skb->sib', inverse_tile, panel_block, precision=precise)  115 us
    all_gather x1, waiting for transfers between devices, local(): second_full = lax.all_gather(masked[:, 1], 'row', axis=1, tiled=True)  82.8 us
    all_gather x1, waiting for transfers between devices, local(): first_full = lax.all_gather(masked[:, 0], 'row', axis=1, tiled=True)  76.2 us
    reduce_scatter x1, waiting for transfers between devices, local(): lax.psum_scatter(tile_product(inverse_tile, shifted), 'col', scatter_dime...  47.1 us
    reduce_scatter x1, waiting for transfers between devices, local(): lax.psum_scatter(tile_product(inverse_tile, first_full), 'col', scatter_d...  36.9 us
    psum x1, waiting for transfers between devices, broadcast(): return lax.psum(block, axis)  21.2 us
    reduce_scatter x1, waiting for transfers between devices, local(): lax.psum_scatter(second_diag_terms, 'row', scatter_dimension=1, tiled=True)  20.5 us
    reduce_scatter x1, waiting for transfers between devices, local(): lax.psum_scatter(first_terms, 'row', scatter_dimension=1, tiled=True)  10.3 us
  transfers between devices with their start and end apart: 9, of which 7 were waited for; matrix products, arithmetic and copies ran while one was open for 33% of the time, Pallas kernels for 0%

commit v1 on v0

v1 whole, which is shorter than its diff:
```python
import jax
import jax.numpy as jnp
from jax import lax
from jax.sharding import PartitionSpec as P

TILE = 128

precise = lax.Precision.HIGH
fine = lax.Precision.HIGHEST


def dot(a, b, contract, precision=precise):
    return lax.dot_general(a, b, ((contract[0:1], contract[1:2]), ((), ())), precision=precision)


def mask_panels(panels, ancestor_tiles):
    rows_axis = lax.axis_size("row")
    local_rows = panels.shape[2]
    row_start = (lax.axis_index("col") * rows_axis + lax.axis_index("row")) * local_rows
    tile_mask = jnp.repeat(ancestor_tiles, TILE, axis=2)
    kept_rows = lax.dynamic_slice_in_dim(tile_mask, row_start, local_rows, 2)
    return jnp.where(kept_rows[..., None] != 0, panels, 0.0)


def own_panels(masked):
    rows_axis, cols_axis = lax.axis_size("row"), lax.axis_size("col")
    pairs = []
    for r in range(rows_axis):
        for c in range(cols_axis):
            block = r * cols_axis + c
            pairs.append(((block % rows_axis) * cols_axis + block // rows_axis, block))
    return lax.ppermute(masked, ("row", "col"), pairs)


def finish(y, own, link, diag_inverse):
    row_id = lax.axis_index("row")
    col_id = lax.axis_index("col")
    height, span = diag_inverse.shape[1:]
    first, second = own[0], own[1]
    y1 = -y[0]
    y2 = -(y[1] + dot(y1, link, (1, 0)))
    shifted = second - dot(first, link, (1, 0))
    link_rows = lax.dynamic_slice_in_dim(link, row_id * height, height, 0)
    link_cols = lax.dynamic_slice_in_dim(link, col_id * span, span, 0)
    given = dot(diag_inverse[0], link_cols, (1, 0))
    f1 = dot(first, y1, (0, 0))
    f2 = dot(first, y2, (0, 0))
    f2 = lax.dynamic_update_slice_in_dim(
        f2, lax.dynamic_slice_in_dim(f2, row_id * height, height, 0) + given, row_id * height, 0
    )
    s2 = dot(shifted, y2, (0, 0)) - dot(link_rows, given, (0, 0))
    terms = jnp.stack([f1, f2, s2])
    terms = lax.psum_scatter(terms, "row", scatter_dimension=1, tiled=True)
    terms = lax.psum_scatter(terms, "col", scatter_dimension=2, tiled=True)
    diag = jnp.stack([diag_inverse[0] - terms[0], diag_inverse[1] - terms[2]])
    return jnp.stack([y1, y2]), diag, -terms[1]


def local(inverse_tile, panels, link_panel, diag_inverse, ancestor_tiles):
    masked = mask_panels(panels, ancestor_tiles)[0]
    own = own_panels(masked)
    ys = []
    for k in range(2):
        full = lax.all_gather(masked[k], "row", axis=0, tiled=True)
        ys.append(lax.psum_scatter(dot(inverse_tile, full, (1, 0)), "col", scatter_dimension=0, tiled=True))
    anc, diag, cross = finish(jnp.stack(ys), own, link_panel[0], diag_inverse[0])
    return anc[None], diag[None], cross[None]


def solution(mesh):
    in_specs = (
        P(("hyp", "row"), "col"),
        P("hyp", None, ("col", "row"), None),
        P("hyp", None, None),
        P("hyp", None, "row", "col"),
        P(),
    )
    out_specs = (
        P("hyp", None, ("row", "col"), None),
        P("hyp", None, "row", "col"),
        P("hyp", "row", "col"),
    )
    return jax.shard_map(local, mesh=mesh, in_specs=in_specs, out_specs=out_specs, check_vma=False)
```

time: 510 us -> 412 us (0.81)
  matrix products: 154 us -> 75.3 us
  blocking collectives: 7.29 us -> 0 us
  other arithmetic: 15.5 us -> 9.23 us
  waiting for transfers between devices: 296 us -> 302 us
    dot_general x8 -> x9, matrix products: 154 us -> 75.3 us  [dot(): lax.dot_general(a, b, ((contract[0:1], contract[1:2]), ((), ())), precisi...]
    reduce_scatter x5 -> x4, waiting for transfers between devices: 115 us -> 169 us  [the longest x2 78.8 us: local(): lax.psum_scatter(dot(inverse_tile, full, (1, 0)), 'col', scatter_dimensio...]
    all_gather x2, waiting for transfers between devices: 159 us -> 132 us  [local(): full = lax.all_gather(masked[k], 'row', axis=0, tiled=True)]
    psum x1 -> x0, waiting for transfers between devices: 21.2 us -> none  [broadcast(): return lax.psum(block, axis)]
    another operation x7 -> x2, other arithmetic: 13.7 us -> 2.05 us  [the longest x1 1.95 us: finish(): terms = jnp.stack([f1, f2, s2])]
    all_gather x1 -> x0, blocking collectives: 7.29 us -> none  [local(): given_rows = lax.all_gather(diag_inverse[:, 0], 'col', axis=2, tiled=True)]
  transfers between devices with their start and end apart: 9 -> 7, of which waited for: 7 -> 6; matrix products, arithmetic and copies ran while one was open for 33% -> 18% of each run, Pallas kernels for 0% -> 0%
where the time goes in v1:
time: 412 us; the launch traced here: 411 us
  waiting for transfers between devices  302 us (73%)
  matrix products  75.3 us (18%)
  between operations  14.3 us (3%)
  other arithmetic  9.23 us (2%)
  local copies, waits for them, and re-layouts  7.71 us (2%)
    all_gather x2, waiting for transfers between devices, local(): full = lax.all_gather(masked[k], 'row', axis=0, tiled=True)  132 us
    reduce_scatter x2, waiting for transfers between devices, local(): lax.psum_scatter(dot(inverse_tile, full, (1, 0)), 'col', scatter_dimensio...  78.8 us
    dot_general x9, matrix products, dot(): lax.dot_general(a, b, ((contract[0:1], contract[1:2]), ((), ())), precisi...  75.3 us
    reduce_scatter x1, waiting for transfers between devices, finish(): terms = lax.psum_scatter(terms, 'row', scatter_dimension=1, tiled=True)  69.5 us
    reduce_scatter x1, waiting for transfers between devices, finish(): terms = lax.psum_scatter(terms, 'col', scatter_dimension=2, tiled=True)  21 us
  transfers between devices with their start and end apart: 7, of which 6 were waited for; matrix products, arithmetic and copies ran while one was open for 18% of the time, Pallas kernels for 0%

profile of v1, /device:TPU:0, one launch (start us, length us, event | category | flops | bytes accessed | tf_op | source)
XLA Modules:
  0.0 411.2 jit_solution(8835298428902315540)
XLA Ops:
  8.2 1.8 broadcast_select_fusion
  10.0 1.5 fusion.30
  12.3 82.8 %all-gather.5.cloned.1.call-done = f32[1,1,2048,512]{3,2,1,0:T(8,128)} async-done(((f32[1,1,512,512]{3,2,1,0:T(8,128)}), f32[1,1,2048,512]{3,2,1,0:T(8,128)}) %all-gather.5.cloned.1.call-update) | async-done | bytes 4194320 | tf_op jit(solution)/shard_map/all_gather | solution.py:64
  95.1 31.4 %fusion.4 = f32[2048,512]{0,1:T(8,128)} fusion(f32[2048,2048]{1,0:T(8,128)} %param.5, f32[1,1,2048,512]{3,2,1,0:T(8,128)} %all-gather.5.cloned.1.call-done), kind=kOutput, calls=%fused_computation.4 | convolution fusion | flops 12884901888 | bytes 25165824 | tf_op jit(solution)/shard_map/dot_general | solution.py:13
  126.7 49.2 %all-gather.7.cloned.1.call-done = f32[1,1,2048,512]{3,2,1,0:T(8,128)} async-done(((f32[1,1,512,512]{3,2,1,0:T(8,128)}), f32[1,1,2048,512]{3,2,1,0:T(8,128)}) %all-gather.7.cloned.1.call-update) | async-done | bytes 4194320 | tf_op jit(solution)/shard_map/all_gather | solution.py:64
  175.9 31.4 %fusion.7 = f32[2048,512]{0,1:T(8,128)} fusion(f32[2048,2048]{1,0:T(8,128)} %param.5, f32[1,1,2048,512]{3,2,1,0:T(8,128)} %all-gather.7.cloned.1.call-done), kind=kOutput, calls=%fused_computation.5 | convolution fusion | flops 12884901888 | bytes 25165824 | tf_op jit(solution)/shard_map/dot_general | solution.py:13
  207.4 1.5 copy-done.4
  208.9 1.5 fusion.36
  210.5 2.2 collective-permute-start
  213.1 0.8 copy.9
  214.0 1.7 fusion.20
  215.6 2.0 fusion.14
  217.6 3.8 reduce-scatter.5.cloned.1.call-done
  221.4 75.1 %reduce-scatter.7.cloned.1.call-done = f32[512,512]{0,1:T(8,128)} async-done(((f32[2048,512]{0,1:T(8,128)}), f32[512,512]{0,1:T(8,128)}) %reduce-scatter.7.cloned.1.call-update) | async-done | bytes 1048592 | tf_op jit(solution)/shard_map/reduce_scatter | solution.py:65
  296.5 2.7 fusion.11
  299.2 1.9 fusion.17
  301.3 1.9 convolution_bitcast_fusion
  303.2 1.9 fusion.10
  305.1 2.0 pad_maximum_fusion
  307.2 69.5 %reduce-scatter.9.cloned.1.call-done = f32[3,128,512]{2,1,0:T(8,128)} async-done(((f32[3,512,512]{2,1,0:T(8,128)}), f32[3,128,512]{2,1,0:T(8,128)}) %reduce-scatter.9.cloned.1.call-update) | async-done | bytes 786448 | tf_op jit(solution)/shard_map/reduce_scatter | solution.py:53
  376.8 1.6 maximum_bitcast_fusion
  378.3 2.9 copy.10
  381.2 21.0 %reduce-scatter.11.cloned.1.call-done = f32[3,128,128]{2,1,0:T(8,128)} async-done(((f32[3,128,512]{2,1,0:T(8,128)}), f32[3,128,128]{2,1,0:T(8,128)}) %reduce-scatter.11.cloned.1.call-update) | async-done | bytes 196624 | tf_op jit(solution)/shard_map/reduce_scatter | solution.py:54
  402.2 1.6 slice_subtract_fusion.1
  (38 shorter events, 3.4 us)
Async XLA Ops:
  7.2 205.6 %copy-start = (f32[1,512,512]{2,1,0:T(8,128)S(1)}, f32[1,512,512]{2,1,0:T(8,128)}, u32[]{:S(2)}) copy-start(f32[1,512,512]{2,1,0:T(8,128)} %param.7) | copy-start | bytes 3145732
  7.2 87.9 %all-gather.5.cloned.1.call-start = ((), (), s32[]{:S(2)}) async-start(), calls=%async_computation.8 | async-start | bytes 5242880 | tf_op jit(solution)/shard_map/all_gather | solution.py:64
  11.5 164.4 %all-gather.7.cloned.1.call-start = ((), (), s32[]{:S(2)}) async-start(), calls=%async_computation.9 | async-start | bytes 5242880 | tf_op jit(solution)/shard_map/all_gather | solution.py:64
  12.2 209.2 %reduce-scatter.5.cloned.1.call-start = ((), (), s32[]{:S(2)}) async-start(), calls=%async_computation.4 | async-start | bytes 5242880 | tf_op jit(solution)/shard_map/reduce_scatter | solution.py:65
  126.5 170.0 %reduce-scatter.7.cloned.1.call-start = ((), (), s32[]{:S(2)}) async-start(), calls=%async_computation.5 | async-start | bytes 5242880 | tf_op jit(solution)/shard_map/reduce_scatter | solution.py:65
  207.3 1.6 copy-start.4
  207.4 5.3 %copy-start.8 = (f32[1,2,128,128]{3,2,1,0:T(8,128)S(1)}, f32[1,2,128,128]{3,2,1,0:T(8,128)}, u32[]{:S(2)}) copy-start(f32[1,2,128,128]{3,2,1,0:T(8,128)} %param.8) | copy-start | bytes 393220
  207.4 169.2 %reduce-scatter.9.cloned.1.call-start = ((), (), s32[]{:S(2)}) async-start(), calls=%async_computation.6 | async-start | bytes 3932160 | tf_op jit(solution)/shard_map/reduce_scatter | solution.py:53
  210.5 5.2 %collective-permute-start = (f32[2,512,512]{2,1,0:T(8,128)}, f32[2,512,512]{2,1,0:T(8,128)S(1)}, u32[]{:S(2)}, u32[]{:S(2)}) collective-permute-start(f32[2,512,512]{2,1,0:T(8,128)} %fusion.36), channel_id=1, source_target_pairs={{0,0},{4,1},{8,2},{12,3},{1,4},{5,5},{9,6},{13,7},{2,8},{6,9},{10,... | collective-permute-start | bytes 6291464 | tf_op jit(solution)/shard_map/ppermute | solution.py:32
  215.6 5.8 %copy-start.2 = (f32[2,512,512]{2,1,0:T(8,128)}, f32[2,512,512]{2,1,0:T(8,128)S(1)}, u32[]{:S(2)}) copy-start(f32[2,512,512]{2,1,0:T(8,128)S(1)} %collective-permute-done) | copy-start | bytes 6291460
  296.5 2.7 copy-start.3
  299.2 2.1 copy-start.7
  299.2 2.1 copy-start.1
  301.2 2.1 copy-start.5
  301.2 2.1 copy-start.6
  307.1 95.1 %reduce-scatter.11.cloned.1.call-start = ((), (), s32[]{:S(2)}) async-start(), calls=%async_computation.7 | async-start | bytes 983040 | tf_op jit(solution)/shard_map/reduce_scatter | solution.py:54
Sparse Core Ops, SparseCore 0:
  11.6 83.4 all-gather.4
  96.7 79.2 all-gather.6
  178.5 42.9 reduce-scatter.4
  223.8 72.6 reduce-scatter.6
  307.2 69.3 reduce-scatter.8
  379.0 23.1 reduce-scatter.10

commit v2 on v1

--- a/solution.py
+++ b/solution.py
@@ -1,12 +1,16 @@
+import functools
+
 import jax
 import jax.numpy as jnp
 from jax import lax
+from jax.experimental import pallas as pl
+from jax.experimental.pallas import tpu as pltpu
 from jax.sharding import PartitionSpec as P
 
 TILE = 128
+MESH = pl.DeviceIdType.MESH
 
 precise = lax.Precision.HIGH
-fine = lax.Precision.HIGHEST
 
 
 def dot(a, b, contract, precision=precise):
@@ -22,14 +26,246 @@
     return jnp.where(kept_rows[..., None] != 0, panels, 0.0)
 
 
-def own_panels(masked):
+def exchange(axis_sizes, chunks, a_hbm, x_hbm, y_ref, own_ref, a_hi, a_lo, stage, p_hi, p_lo, gathered, partial,
+             received, own, stage_sem, load_sem, send_sem, recv_sem, part_send, part_recv, own_send, own_recv, own_local):
+    rows_axis, cols_axis = axis_sizes
+    r = lax.axis_index("row")
+    c = lax.axis_index("col")
+    _, _, rows, width = gathered.shape
+    half = rows // 2
+    per_panel = chunks // x_hbm.shape[0]
+    pieces = 2 * (rows_axis - 1)
+    tile = stage.shape[1]
+    tiles = a_hbm.shape[0] // tile
+
+    def load(q):
+        src = x_hbm.at[q // per_panel, :, pl.ds((q % per_panel) * width, width)]
+        return pltpu.make_async_copy(src, gathered.at[q, r], load_sem.at[q])
+
+    def stage_copy(i):
+        src = a_hbm.at[pl.ds(pl.multiple_of(i * tile, tile), tile)]
+        return pltpu.make_async_copy(src, stage.at[i % 2], stage_sem.at[i % 2])
+
+    def hop(q, block, h, way, target):
+        ref = gathered.at[q, block, pl.ds(pl.multiple_of(h * half, half), half)]
+        return pltpu.make_async_remote_copy(
+            ref, ref, send_sem.at[way, q, block, h], recv_sem.at[q, block, h],
+            device_id={"row": target}, device_id_type=MESH)
+
+    def each_send(q, s, h, act):
+        @pl.when((r + 1 < rows_axis) & (r - s >= 0))
+        def _():
+            act(hop(q, r - s, h, 0, r + 1))
+
+        @pl.when((r >= 1) & (r + s < rows_axis))
+        def _():
+            act(hop(q, r + s, h, 1, r - 1))
+
+    def wait_arrivals(q, s, h):
+        @pl.when(r - 1 - s >= 0)
+        def _():
+            hop(q, r - 1 - s, h, 0, r - 1).wait_recv()
+
+        @pl.when(r + 1 + s < rows_axis)
+        def _():
+            hop(q, r + 1 + s, h, 1, r + 1).wait_recv()
+
+    def part(q, target, source):
+        return pltpu.make_async_remote_copy(
+            partial.at[q, target], received.at[q, source], part_send.at[q, target], part_recv.at[q, source],
+            device_id={"col": target}, device_id_type=MESH)
+
+    def own_copy(q, target):
+        return pltpu.make_async_remote_copy(
+            gathered.at[q, (r * cols_axis + target) % rows_axis], own.at[q], own_send.at[q, target], own_recv.at[q],
+            device_id={"col": target}, device_id_type=MESH)
+
+    def own_here(q):
+        return pltpu.make_async_copy(gathered.at[q, (r * cols_axis + c) % rows_axis], own.at[q], own_local.at[q])
+
+    own_root = (r * cols_axis + c) // rows_axis
+
+    def each_own(q, act):
+        for shift in range(1, cols_axis):
+            target = (c + shift) % cols_axis
+
+            @pl.when((r * cols_axis + target) // rows_axis == c)
+            def _():
+                act(own_copy(q, target))
+
+    for q in range(chunks):
+        load(q).start()
+    stage_copy(0).start()
+    barrier = pltpu.get_barrier_semaphore()
+    for shift in range(1, cols_axis):
+        pl.semaphore_signal(barrier, inc=1, device_id={"col": (c + shift) % cols_axis}, device_id_type=MESH)
+
+    @pl.when(r >= 1)
+    def _():
+        pl.semaphore_signal(barrier, inc=1, device_id={"row": r - 1}, device_id_type=MESH)
+
+    @pl.when(r + 1 < rows_axis)
+    def _():
+        pl.semaphore_signal(barrier, inc=1, device_id={"row": r + 1}, device_id_type=MESH)
+
+    inner = (r >= 1) & (r + 1 < rows_axis)
+
+    @pl.when(inner)
+    def _():
+        pl.semaphore_wait(barrier, cols_axis + 1)
+
+    @pl.when(jnp.logical_not(inner))
+    def _():
+        pl.semaphore_wait(barrier, cols_axis)
+
+    for q in range(chunks):
+        load(q).wait()
+
+    def split_tile(i, carry):
+        @pl.when(i + 1 < tiles)
+        def _():
+            stage_copy(i + 1).start()
+
+        stage_copy(i).wait()
+        at = pl.ds(pl.multiple_of(i * tile, tile), tile)
+        value = stage[i % 2]
+        high = value.astype(jnp.bfloat16)
+        a_hi[at, :] = high
+        a_lo[at, :] = (value - high.astype(jnp.float32)).astype(jnp.bfloat16)
+        return carry
+
+    def multiply(k, i):
+        even = 1 - 2 * (c % 2)
+        target = (c + cols_axis // 2 + even * i + cols_axis) % cols_axis
+        at = pl.ds(pl.multiple_of(target * rows, rows), rows)
+        high = a_hi[at, :]
+        out = jnp.dot(high, p_hi[...], preferred_element_type=jnp.float32)
+        out += jnp.dot(high, p_lo[...], preferred_element_type=jnp.float32)
+        out += jnp.dot(a_lo[at, :], p_hi[...], preferred_element_type=jnp.float32)
+        partial[k, target] = out
+
+        @pl.when(target != c)
+        def _():
+            part(k, target, c).start()
+
+    def step(u, carry):
+        q, p = u // pieces, u % pieces
+        s, h = p // 2, p % 2
+
+        @pl.when((u >= 2) & (u < chunks * pieces + 2))
+        def _():
+            v = u - 2
+            wait_arrivals(v // pieces, (v % pieces) // 2, v % 2)
+
+        @pl.when(q < chunks)
+        def _():
+            each_send(q, s, h, lambda copy: copy.start())
+
+        @pl.when(u == 1)
+        def _():
+            lax.fori_loop(0, tiles, split_tile, 0)
+
+        @pl.when((q >= 1) & (p == 1))
+        def _():
+            k = q - 1
+            each_own(k, lambda copy: copy.start())
+
+            @pl.when(own_root == c)
+            def _():
+                own_here(k).start()
+
+            def split_panel(b, carry):
+                at = pl.ds(pl.multiple_of(b * rows, rows), rows)
+                value = gathered[k, b]
+                high = value.astype(jnp.bfloat16)
+                p_hi[at, :] = high
+                p_lo[at, :] = (value - high.astype(jnp.float32)).astype(jnp.bfloat16)
+                return carry
+
+            lax.fori_loop(0, rows_axis, split_panel, 0)
+
+        @pl.when((q >= 1) & (p >= 1))
+        def _():
+            def body(i, carry):
+                multiply(q - 1, i)
+                return carry
+
+            lax.fori_loop((p - 1) * cols_axis // (pieces - 1), p * cols_axis // (pieces - 1), body, 0)
+
+        return carry
+
+    lax.fori_loop(0, (chunks + 1) * pieces, step, 0)
+
+    for q in range(chunks):
+        panel, start = q // per_panel, (q % per_panel) * width
+        at = (panel, slice(None), slice(start, start + width))
+        total = partial[q, c]
+        for shift in range(1, cols_axis):
+            source = (c + shift) % cols_axis
+            part(q, source, source).wait_recv()
+            total += received[q, source]
+        y_ref[at] = total
+
+        @pl.when(own_root == c)
+        def _():
+            own_here(q).wait()
+
+        @pl.when(own_root != c)
+        def _():
+            own_copy(q, own_root).wait_recv()
+
+        own_ref[at] = own[q]
+
+    def drain(u, carry):
+        q, p = u // pieces, u % pieces
+        each_send(q, p // 2, p % 2, lambda copy: copy.wait_send())
+        return carry
+
+    lax.fori_loop(0, chunks * pieces, drain, 0)
+    for q in range(chunks):
+        each_own(q, lambda copy: copy.wait_send())
+        for shift in range(1, cols_axis):
+            part(q, (c + shift) % cols_axis, c).wait_send()
+
+
+def products(inverse_tile, masked):
     rows_axis, cols_axis = lax.axis_size("row"), lax.axis_size("col")
-    pairs = []
-    for r in range(rows_axis):
-        for c in range(cols_axis):
-            block = r * cols_axis + c
-            pairs.append(((block % rows_axis) * cols_axis + block // rows_axis, block))
-    return lax.ppermute(masked, ("row", "col"), pairs)
+    height, depth = inverse_tile.shape
+    count, rows, columns = masked.shape
+    width = min(256, columns)
+    chunks = count * columns // width
+    tile = min(128, height)
+    f32, bf16 = jnp.float32, jnp.bfloat16
+    dma = pltpu.SemaphoreType.DMA
+    result = jax.ShapeDtypeStruct((count, rows, columns), f32)
+    return pl.pallas_call(
+        functools.partial(exchange, (rows_axis, cols_axis), chunks),
+        out_shape=(result, result),
+        in_specs=[pl.BlockSpec(memory_space=pl.ANY)] * 2,
+        out_specs=[pl.BlockSpec(memory_space=pltpu.VMEM)] * 2,
+        scratch_shapes=[
+            pltpu.VMEM((height, depth), bf16),
+            pltpu.VMEM((height, depth), bf16),
+            pltpu.VMEM((2, tile, depth), f32),
+            pltpu.VMEM((depth, width), bf16),
+            pltpu.VMEM((depth, width), bf16),
+            pltpu.VMEM((chunks, rows_axis, rows, width), f32),
+            pltpu.VMEM((chunks, cols_axis, rows, width), f32),
+            pltpu.VMEM((chunks, cols_axis, rows, width), f32),
+            pltpu.VMEM((chunks, rows, width), f32),
+            dma((2,)),
+            dma((chunks,)),
+            dma((2, chunks, rows_axis, 2)),
+            dma((chunks, rows_axis, 2)),
+            dma((chunks, cols_axis)),
+            dma((chunks, cols_axis)),
+            dma((chunks, cols_axis)),
+            dma((chunks,)),
+            dma((chunks,)),
+        ],
+        compiler_params=pltpu.CompilerParams(
+            collective_id=0, has_side_effects=True, vmem_limit_bytes=60 * 1024 * 1024),
+    )(inverse_tile, masked)
 
 
 def finish(y, own, link, diag_inverse):
@@ -58,12 +294,8 @@
 
 def local(inverse_tile, panels, link_panel, diag_inverse, ancestor_tiles):
     masked = mask_panels(panels, ancestor_tiles)[0]
-    own = own_panels(masked)
-    ys = []
-    for k in range(2):
-        full = lax.all_gather(masked[k], "row", axis=0, tiled=True)
-        ys.append(lax.psum_scatter(dot(inverse_tile, full, (1, 0)), "col", scatter_dimension=0, tiled=True))
-    anc, diag, cross = finish(jnp.stack(ys), own, link_panel[0], diag_inverse[0])
+    ys, own = products(inverse_tile, masked)
+    anc, diag, cross = finish(ys, own, link_panel[0], diag_inverse[0])
     return anc[None], diag[None], cross[None]
 
 

time: 412 us -> 302 us (0.73)
  waiting for transfers between devices: 302 us -> 83 us
  Pallas kernels: 0 us -> 180 us
  matrix products: 75.3 us -> 9.76 us
  local copies, waits for them, and re-layouts: 7.71 us -> 3.26 us
    pallas_call x0 -> x1, Pallas kernels: none -> 180 us  [products(): pl.pallas_call(functools.partial(exchange, (rows_axis, cols_axis), chunks...]
    all_gather x2 -> x0, waiting for transfers between devices: 132 us -> none  [local(): full = lax.all_gather(masked[k], 'row', axis=0, tiled=True)]
    reduce_scatter x2 -> x0, waiting for transfers between devices: 78.8 us -> none  [local(): lax.psum_scatter(dot(inverse_tile, full, (1, 0)), 'col', scatter_dimensio...]
    dot_general x9 -> x7, matrix products: 75.3 us -> 9.76 us  [dot(): lax.dot_general(a, b, ((contract[0:1], contract[1:2]), ((), ())), precisi...]
    reduce_scatter x1, waiting for transfers between devices: 69.5 us -> 60.2 us  [finish(): terms = lax.psum_scatter(terms, 'row', scatter_dimension=1, tiled=True)]
  transfers between devices with their start and end apart: 7 -> 2, of which waited for: 6 -> 2; matrix products, arithmetic and copies ran while one was open for 18% -> 1% of each run, Pallas kernels for 0% -> 0%
where the time goes in v2:
time: 302 us
  Pallas kernels  180 us (60%)
  waiting for transfers between devices  83 us (27%)
  between operations  14.2 us (5%)
  other arithmetic  11.9 us (4%)
  matrix products  9.76 us (3%)
  local copies, waits for them, and re-layouts  3.26 us (1%)
    pallas_call x1, Pallas kernels, products(): pl.pallas_call(functools.partial(exchange, (rows_axis, cols_axis), chunks...  180 us
    reduce_scatter x1, waiting for transfers between devices, finish(): terms = lax.psum_scatter(terms, 'row', scatter_dimension=1, tiled=True)  60.2 us
    reduce_scatter x1, waiting for transfers between devices, finish(): terms = lax.psum_scatter(terms, 'col', scatter_dimension=2, tiled=True)  22.8 us
    dot_general x7, matrix products, dot(): lax.dot_general(a, b, ((contract[0:1], contract[1:2]), ((), ())), precisi...  9.76 us
  transfers between devices with their start and end apart: 2, of which 2 were waited for; matrix products, arithmetic and copies ran while one was open for 1% of the time, Pallas kernels for 0%

profile of v2, /device:TPU:0, one launch (start us, length us, event | category | flops | bytes accessed | tf_op | source)
XLA Modules:
  0.0 301.7 jit_solution(13828007340841521445)
XLA Ops:
  7.2 0.8 broadcast_bitcast_fusion
  8.1 0.1 copy.11
  8.2 3.1 %select_bitcast_fusion.x_hbm = f32[2,512,512]{2,1,0:T(8,128)} fusion(f32[1,2,512,512]{3,2,1,0:T(8,128)} %param.6, pred[2,512]{1,0:T(4,128)(4,1)S(1)} %dynamic-slice_compare_fusion), kind=kLoop, calls=%fused_computation.2 | loop fusion | flops 524288 | bytes 4195328 | tf_op jit(solution)/shard_map/squeeze | solution.py:296
  11.3 179.6 %shard_map.79 = (f32[2,512,512]{2,1,0:T(8,128)}, f32[2,512,512]{2,1,0:T(8,128)}) custom-call(f32[2048,2048]{1,0:T(8,128)} %a_hbm.1, f32[2,512,512]{2,1,0:T(8,128)} %select_bitcast_fusion.x_hbm), custom_call_target="tpu_custom_call" | custom-call | tf_op jit(solution)/shard_map/pallas_call | solution.py:241
  191.0 2.7 fusion.1
  193.7 2.0 convolution_subtract_fusion.1
  195.7 2.0 convolution_bitcast_fusion
  197.7 1.0 fusion.3
  198.7 1.0 copy.12
  199.7 0.4 fusion.15
  200.1 0.8 copy.8
  201.0 0.6 fusion.13
  201.6 1.7 bitcast_dynamic-update-slice_fusion
  203.3 1.0 fusion
  204.3 0.2 copy-done.3
  204.5 0.3 copy-done.5
  204.8 1.9 pad_maximum_fusion
  206.8 0.0 reduce-scatter.5.cloned.1.call-start
  206.8 60.2 %reduce-scatter.3.cloned.1.call-done = f32[3,128,512]{2,1,0:T(8,128)} async-done(((f32[3,512,512]{2,1,0:T(8,128)}), f32[3,128,512]{2,1,0:T(8,128)}) %reduce-scatter.3.cloned.1.call-update) | async-done | bytes 786448 | tf_op jit(solution)/shard_map/reduce_scatter | solution.py:289
  267.0 1.3 slice_negate_fusion
  268.4 1.5 maximum_bitcast_fusion
  269.9 22.8 %reduce-scatter.5.cloned.1.call-done = f32[3,128,128]{2,1,0:T(8,128)} async-done(((f32[3,128,512]{2,1,0:T(8,128)}), f32[3,128,128]{2,1,0:T(8,128)}) %reduce-scatter.5.cloned.1.call-update) | async-done | bytes 196624 | tf_op jit(solution)/shard_map/reduce_scatter | solution.py:290
  292.7 1.6 slice_subtract_fusion.1
  294.2 0.7 maximum_bitcast_fusion.1
  (16 shorter events, 0.1 us)
Async XLA Ops:
  7.2 183.8 %copy-start = (f32[1,512,512]{2,1,0:T(8,128)S(1)}, f32[1,512,512]{2,1,0:T(8,128)}, u32[]{:S(2)}) copy-start(f32[1,512,512]{2,1,0:T(8,128)} %param.7) | copy-start | bytes 3145732
  7.2 259.8 %reduce-scatter.3.cloned.1.call-start = ((), (), s32[]{:S(2)}) async-start(), calls=%async_computation.2 | async-start | bytes 3932160 | tf_op jit(solution)/shard_map/reduce_scatter | solution.py:289
  190.9 2.7 copy-start.1
  193.7 2.0 copy-start.2
  197.7 2.1 copy-start.6
  201.0 2.3 copy-start.4
  203.3 1.2 copy-start.3
  203.3 1.5 copy-start.5
  206.8 85.9 %reduce-scatter.5.cloned.1.call-start = ((), (), s32[]{:S(2)}) async-start(), calls=%async_computation.3 | async-start | bytes 983040 | tf_op jit(solution)/shard_map/reduce_scatter | solution.py:290
Sparse Core Ops, SparseCore 0:
  206.9 60.0 reduce-scatter.2
  269.5 23.1 reduce-scatter.4

commit v3 on v2

--- a/solution.py
+++ b/solution.py
@@ -268,6 +268,82 @@
     )(inverse_tile, masked)
 
 
+def halving_levels():
+    levels = []
+    for axis in ("col", "row"):
+        dist = 1
+        while dist < lax.axis_size(axis):
+            levels.append((axis, dist))
+            dist *= 2
+    return levels
+
+
+def halve(levels, count, terms, out_ref, *scratch):
+    depth = len(levels)
+    kept = (terms,) + scratch[: depth - 1]
+    landed = scratch[depth - 1 : 2 * depth - 1]
+    send_sem, recv_sem = scratch[2 * depth - 1 :]
+
+    def bit_and_partner(level):
+        axis, dist = levels[level]
+        at = lax.axis_index(axis)
+        bit = (at // dist) % 2
+        return bit, {axis: at + dist * (1 - 2 * bit)}
+
+    def copy(level, k):
+        bit, partner = bit_and_partner(level)
+        return pltpu.make_async_remote_copy(
+            kept[level].at[k, :, 1 - bit], landed[level].at[k], send_sem.at[level, k], recv_sem.at[level, k],
+            device_id=partner, device_id_type=MESH)
+
+    barrier = pltpu.get_barrier_semaphore()
+    for level in range(depth):
+        pl.semaphore_signal(barrier, inc=1, device_id=bit_and_partner(level)[1], device_id_type=MESH)
+    pl.semaphore_wait(barrier, depth)
+
+    for level in range(depth + 1):
+        for k in range(count):
+            if level > 0:
+                copy(level - 1, k).wait_recv()
+                bit, _ = bit_and_partner(level - 1)
+                total = kept[level - 1][k, :, bit] + landed[level - 1][k]
+                target = kept[level] if level < depth else out_ref
+                target[k] = total.reshape(target.shape[1:])
+            if level < depth:
+                copy(level, k).start()
+    for level in range(depth):
+        for k in range(count):
+            copy(level, k).wait_send()
+
+
+def reduce_blocks(terms, height, span):
+    rows_axis, cols_axis = lax.axis_size("row"), lax.axis_size("col")
+    count = terms.shape[0]
+    terms = terms.reshape(count, rows_axis, height, cols_axis, span).transpose(0, 3, 1, 2, 4)
+    levels = halving_levels()
+    shapes = []
+    cols, rows = cols_axis, rows_axis
+    for axis, _ in levels:
+        if axis == "col":
+            cols //= 2
+            shapes.append(((cols, 2, rows, height, span), (cols, rows, height, span)))
+        else:
+            rows //= 2
+            shapes.append(((rows, 2, height, span), (rows, height, span)))
+    dma = pltpu.SemaphoreType.DMA((len(levels), count))
+    return pl.pallas_call(
+        functools.partial(halve, levels, count),
+        out_shape=jax.ShapeDtypeStruct((count, height, span), jnp.float32),
+        in_specs=[pl.BlockSpec(memory_space=pltpu.VMEM)],
+        out_specs=pl.BlockSpec(memory_space=pltpu.VMEM),
+        scratch_shapes=[pltpu.VMEM((count,) + kept, jnp.float32) for kept, _ in shapes[1:]]
+        + [pltpu.VMEM((count,) + landed, jnp.float32) for _, landed in shapes]
+        + [dma, dma],
+        compiler_params=pltpu.CompilerParams(
+            collective_id=1, has_side_effects=True, vmem_limit_bytes=32 * 1024 * 1024),
+    )(terms.reshape((count,) + shapes[0][0]))
+
+
 def finish(y, own, link, diag_inverse):
     row_id = lax.axis_index("row")
     col_id = lax.axis_index("col")
@@ -286,8 +362,7 @@
     )
     s2 = dot(shifted, y2, (0, 0)) - dot(link_rows, given, (0, 0))
     terms = jnp.stack([f1, f2, s2])
-    terms = lax.psum_scatter(terms, "row", scatter_dimension=1, tiled=True)
-    terms = lax.psum_scatter(terms, "col", scatter_dimension=2, tiled=True)
+    terms = reduce_blocks(terms, height, span)
     diag = jnp.stack([diag_inverse[0] - terms[0], diag_inverse[1] - terms[2]])
     return jnp.stack([y1, y2]), diag, -terms[1]
 

time: 302 us -> 248 us (0.82)
  waiting for transfers between devices: 83 us -> 0 us
  Pallas kernels: 180 us -> 211 us
  between operations: 14.2 us -> 0.84 us
  local copies, waits for them, and re-layouts: 3.26 us -> 15.7 us
    reduce_scatter x2 -> x0, waiting for transfers between devices: 83 us -> none  [the longest x1 60.2 us: finish(): terms = lax.psum_scatter(terms, 'row', scatter_dimension=1, tiled=True)]
    pallas_call x0 -> x1, Pallas kernels: none -> 31.8 us  [reduce_blocks(): pl.pallas_call(functools.partial(halve, levels, count), out_shape=jax.Sha...]
    another operation x0 -> x5, local copies, waits for them, and re-layouts: none -> 7.89 us  [the longest x4 5.34 us: finish(): terms = jnp.stack([f1, f2, s2])]
    dot_general x1 -> x3, local copies, waits for them, and re-layouts: 0.83 us -> 4.65 us  [dot(): lax.dot_general(a, b, ((contract[0:1], contract[1:2]), ((), ())), precisi...]
  transfers between devices with their start and end apart: 2 -> 0, of which waited for: 2 -> 0; matrix products, arithmetic and copies ran while one was open for 1% -> 0% of each run, Pallas kernels for 0% -> 0%
where the time goes in v3:
time: 248 us
  Pallas kernels  211 us (85%)
  local copies, waits for them, and re-layouts  15.7 us (6%)
  matrix products  10.1 us (4%)
  other arithmetic  9.58 us (4%)
    pallas_call x1, Pallas kernels, products(): pl.pallas_call(functools.partial(exchange, (rows_axis, cols_axis), chunks...  180 us
    pallas_call x1, Pallas kernels, reduce_blocks(): pl.pallas_call(functools.partial(halve, levels, count), out_shape=jax.Sha...  31.8 us
    dot_general x7, matrix products, dot(): lax.dot_general(a, b, ((contract[0:1], contract[1:2]), ((), ())), precisi...  10.1 us
    another operation x4, local copies, waits for them, and re-layouts, finish(): terms = jnp.stack([f1, f2, s2])  5.34 us

profile of v3, /device:TPU:0, one launch (start us, length us, event | category | flops | bytes accessed | tf_op | source)
XLA Modules:
  0.0 247.7 jit_solution(5302496978873642093)
XLA Ops:
  0.7 0.8 broadcast_bitcast_fusion
  1.6 3.1 %select_bitcast_fusion.x_hbm = f32[2,512,512]{2,1,0:T(8,128)} fusion(f32[1,2,512,512]{3,2,1,0:T(8,128)} %param.6, pred[2,512]{1,0:T(4,128)(4,1)S(1)} %dynamic-slice_compare_fusion), kind=kLoop, calls=%fused_computation.2 | loop fusion | flops 524288 | bytes 4195328 | tf_op jit(solution)/shard_map/squeeze | solution.py:371
  4.7 179.6 %shard_map.79 = (f32[2,512,512]{2,1,0:T(8,128)}, f32[2,512,512]{2,1,0:T(8,128)}) custom-call(f32[2048,2048]{1,0:T(8,128)} %a_hbm.1, f32[2,512,512]{2,1,0:T(8,128)} %select_bitcast_fusion.x_hbm), custom_call_target="tpu_custom_call" | custom-call | tf_op jit(solution)/shard_map/pallas_call | solution.py:241
  184.4 2.7 %fusion = f32[512,512]{1,0:T(8,128)S(1)} fusion(f32[1,512,512]{2,1,0:T(8,128)S(1)} %copy-done, f32[2,512,512]{2,1,0:T(8,128)} %get-tuple-element.5), kind=kOutput, calls=%fused_computation.7 | convolution fusion | flops 806092800 | bytes 4194304 | tf_op jit(solution)/shard_map/dot_general | solution.py:17
  187.1 1.0 fusion.1
  188.1 1.0 copy.24
  189.5 0.8 copy.14
  190.4 1.7 bitcast_dynamic-update-slice_fusion
  192.0 1.6 stack.30
  193.6 1.1 copy.15
  195.6 1.0 convolution_subtract_fusion.1
  196.6 2.0 convolution_subtract_fusion
  198.6 1.6 stack.31
  200.2 1.1 copy.16
  201.3 0.9 copy-done.6
  202.1 1.6 fusion.19
  203.7 1.6 copy.20
  205.3 2.3 slice_bitcast_fusion
  207.5 2.5 %copy.19 = f32[512,512]{1,0:T(8,128)} copy(f32[512,512]{0,1:T(8,128)} %slice_bitcast_fusion) | data formatting | bytes 2097152 | tf_op jit(solution)/shard_map/reshape.37
  210.1 2.4 convolution_bitcast_fusion
  213.1 31.8 %shard_map.80 = f32[3,128,128]{2,1,0:T(8,128)S(1)} custom-call(f32[3,2,2,4,128,128]{5,4,3,2,1,0:T(8,128)S(1)} %bitcast.75), custom_call_target="tpu_custom_call" | custom-call | tf_op jit(solution)/shard_map/pallas_call | solution.py:334
  244.9 0.7 bitcast_subtract_fusion.1
  245.5 0.7 maximum_bitcast_fusion.2
  246.2 1.5 maximum_bitcast_fusion.1
  (21 shorter events, 1.9 us)
Async XLA Ops:
  0.6 183.7 %copy-start = (f32[1,512,512]{2,1,0:T(8,128)S(1)}, f32[1,512,512]{2,1,0:T(8,128)}, u32[]{:S(2)}) copy-start(f32[1,512,512]{2,1,0:T(8,128)} %param.7) | copy-start | bytes 3145732
  184.4 2.7 %copy-start.1 = (f32[2,512,512]{2,1,0:T(8,128)S(1)}, f32[2,512,512]{2,1,0:T(8,128)}, u32[]{:S(2)}) copy-start(f32[2,512,512]{2,1,0:T(8,128)} %get-tuple-element.6) | copy-start | bytes 6291460
  187.1 2.0 copy-start.7
  193.6 2.0 copy-start.2
  200.2 2.0 copy-start.6
  210.1 2.4 copy-start.4
  210.1 2.4 copy-start.5
  213.1 33.1 %copy-start.3 = (f32[1,512,512]{2,1,0:T(8,128)S(1)}, f32[1,512,512]{2,1,0:T(8,128)}, u32[]{:S(2)}) copy-start(f32[1,512,512]{2,1,0:T(8,128)} %get-tuple-element.8) | copy-start | bytes 3145732

commit v4 on v3

--- a/solution.py
+++ b/solution.py
@@ -9,12 +9,6 @@
 
 TILE = 128
 MESH = pl.DeviceIdType.MESH
-
-precise = lax.Precision.HIGH
-
-
-def dot(a, b, contract, precision=precise):
-    return lax.dot_general(a, b, ((contract[0:1], contract[1:2]), ((), ())), precision=precision)
 
 
 def mask_panels(panels, ancestor_tiles):
@@ -278,8 +272,23 @@
     return levels
 
 
-def halve(levels, count, terms, out_ref, *scratch):
+def split(value):
+    high = value.astype(jnp.bfloat16)
+    return high, (value - high.astype(jnp.float32)).astype(jnp.bfloat16)
+
+
+def dot3(a, b, contract):
+    def one(left, right):
+        return lax.dot_general(
+            left, right, (((contract,), (0,)), ((), ())), preferred_element_type=jnp.float32)
+
+    return one(a[0], b[0]) + (one(a[0], b[1]) + one(a[1], b[0]))
+
+
+def finish_kernel(levels, count, y_ref, own_ref, link_ref, given_ref, anc_ref, diag_ref, cross_ref, terms, out_ref, *scratch):
     depth = len(levels)
+    height, span = given_ref.shape[1:]
+    rows_axis, cols_axis = terms.shape[3], 2 * terms.shape[1]
     kept = (terms,) + scratch[: depth - 1]
     landed = scratch[depth - 1 : 2 * depth - 1]
     send_sem, recv_sem = scratch[2 * depth - 1 :]
@@ -301,25 +310,54 @@
         pl.semaphore_signal(barrier, inc=1, device_id=bit_and_partner(level)[1], device_id_type=MESH)
     pl.semaphore_wait(barrier, depth)
 
-    for level in range(depth + 1):
+    def store(k, value):
+        for col in range(cols_axis):
+            for row in range(rows_axis):
+                terms[k, col // 2, col % 2, row] = value[
+                    row * height : (row + 1) * height, col * span : (col + 1) * span]
+
+    row_id, col_id = lax.axis_index("row"), lax.axis_index("col")
+    y1 = -y_ref[0]
+    anc_ref[0] = y1
+    first, y1_parts = split(own_ref[0]), split(y1)
+    store(0, dot3(first, y1_parts, 0))
+    copy(0, 0).start()
+    link = split(link_ref[...])
+    link_cols = link_ref[pl.ds(pl.multiple_of(col_id * span, span), span), :]
+    link_rows = link_ref[pl.ds(pl.multiple_of(row_id * height, height), height), :]
+    given = dot3(split(given_ref[0]), split(link_cols), 1)
+    y2 = -(y_ref[1] + dot3(y1_parts, link, 1))
+    anc_ref[1] = y2
+    y2_parts = split(y2)
+    store(1, dot3(first, y2_parts, 0))
+    for col in range(cols_axis):
+        terms[1, col // 2, col % 2, row_id] += given[:, col * span : (col + 1) * span]
+    copy(0, 1).start()
+    shifted = split(own_ref[1] - dot3(first, link, 1))
+    store(2, dot3(shifted, y2_parts, 0) - dot3(split(link_rows), split(given), 0))
+    copy(0, 2).start()
+
+    for level in range(1, depth + 1):
         for k in range(count):
-            if level > 0:
-                copy(level - 1, k).wait_recv()
-                bit, _ = bit_and_partner(level - 1)
-                total = kept[level - 1][k, :, bit] + landed[level - 1][k]
-                target = kept[level] if level < depth else out_ref
-                target[k] = total.reshape(target.shape[1:])
+            copy(level - 1, k).wait_recv()
+            bit, _ = bit_and_partner(level - 1)
+            total = kept[level - 1][k, :, bit] + landed[level - 1][k]
+            target = kept[level] if level < depth else out_ref
+            target[k] = total.reshape(target.shape[1:])
             if level < depth:
                 copy(level, k).start()
+    diag_ref[0] = given_ref[0] - out_ref[0]
+    diag_ref[1] = given_ref[1] - out_ref[2]
+    cross_ref[...] = -out_ref[1]
     for level in range(depth):
         for k in range(count):
             copy(level, k).wait_send()
 
 
-def reduce_blocks(terms, height, span):
+def finish(y, own, link, given):
     rows_axis, cols_axis = lax.axis_size("row"), lax.axis_size("col")
-    count = terms.shape[0]
-    terms = terms.reshape(count, rows_axis, height, cols_axis, span).transpose(0, 3, 1, 2, 4)
+    count = 3
+    height, span = given.shape[1:]
     levels = halving_levels()
     shapes = []
     cols, rows = cols_axis, rows_axis
@@ -332,39 +370,24 @@
             shapes.append(((rows, 2, height, span), (rows, height, span)))
     dma = pltpu.SemaphoreType.DMA((len(levels), count))
     return pl.pallas_call(
-        functools.partial(halve, levels, count),
-        out_shape=jax.ShapeDtypeStruct((count, height, span), jnp.float32),
-        in_specs=[pl.BlockSpec(memory_space=pltpu.VMEM)],
-        out_specs=pl.BlockSpec(memory_space=pltpu.VMEM),
-        scratch_shapes=[pltpu.VMEM((count,) + kept, jnp.float32) for kept, _ in shapes[1:]]
+        functools.partial(finish_kernel, levels, count),
+        out_shape=(
+            jax.ShapeDtypeStruct(y.shape, jnp.float32),
+            jax.ShapeDtypeStruct(given.shape, jnp.float32),
+            jax.ShapeDtypeStruct((height, span), jnp.float32),
+        ),
+        in_specs=[pl.BlockSpec(memory_space=pltpu.VMEM)] * 4,
+        out_specs=[pl.BlockSpec(memory_space=pltpu.VMEM)] * 3,
+        scratch_shapes=[
+            pltpu.VMEM((count,) + shapes[0][0], jnp.float32),
+            pltpu.VMEM((count, height, span), jnp.float32),
+        ]
+        + [pltpu.VMEM((count,) + kept, jnp.float32) for kept, _ in shapes[1:]]
         + [pltpu.VMEM((count,) + landed, jnp.float32) for _, landed in shapes]
         + [dma, dma],
         compiler_params=pltpu.CompilerParams(
-            collective_id=1, has_side_effects=True, vmem_limit_bytes=32 * 1024 * 1024),
-    )(terms.reshape((count,) + shapes[0][0]))
-
-
-def finish(y, own, link, diag_inverse):
-    row_id = lax.axis_index("row")
-    col_id = lax.axis_index("col")
-    height, span = diag_inverse.shape[1:]
-    first, second = own[0], own[1]
-    y1 = -y[0]
-    y2 = -(y[1] + dot(y1, link, (1, 0)))
-    shifted = second - dot(first, link, (1, 0))
-    link_rows = lax.dynamic_slice_in_dim(link, row_id * height, height, 0)
-    link_cols = lax.dynamic_slice_in_dim(link, col_id * span, span, 0)
-    given = dot(diag_inverse[0], link_cols, (1, 0))
-    f1 = dot(first, y1, (0, 0))
-    f2 = dot(first, y2, (0, 0))
-    f2 = lax.dynamic_update_slice_in_dim(
-        f2, lax.dynamic_slice_in_dim(f2, row_id * height, height, 0) + given, row_id * height, 0
-    )
-    s2 = dot(shifted, y2, (0, 0)) - dot(link_rows, given, (0, 0))
-    terms = jnp.stack([f1, f2, s2])
-    terms = reduce_blocks(terms, height, span)
-    diag = jnp.stack([diag_inverse[0] - terms[0], diag_inverse[1] - terms[2]])
-    return jnp.stack([y1, y2]), diag, -terms[1]
+            collective_id=1, has_side_effects=True, vmem_limit_bytes=48 * 1024 * 1024),
+    )(y, own, link, given)
 
 
 def local(inverse_tile, panels, link_panel, diag_inverse, ancestor_tiles):

time: 248 us -> 226 us (0.911)
  local copies, waits for them, and re-layouts: 15.7 us -> 5 us
  matrix products: 10.1 us -> 0 us
  other arithmetic: 9.58 us -> 3.15 us
  Pallas kernels: 211 us -> 215 us
    dot_general x7 -> x0, matrix products: 10.1 us -> none  [dot(): lax.dot_general(a, b, ((contract[0:1], contract[1:2]), ((), ())), precisi...]
    another operation x5 -> x0, local copies, waits for them, and re-layouts: 7.89 us -> none  [the longest x4 5.34 us: finish(): terms = jnp.stack([f1, f2, s2])]
    dot_general x3 -> x0, local copies, waits for them, and re-layouts: 4.65 us -> none  [dot(): lax.dot_general(a, b, ((contract[0:1], contract[1:2]), ((), ())), precisi...]
    pallas_call x1, Pallas kernels: 31.8 us -> 35.2 us  [finish(): pl.pallas_call(functools.partial(finish_kernel, levels, count), out_shape...]
    unnamed x19 -> x13, local copies, waits for them, and re-layouts: 2.98 us -> 5 us
where the time goes in v4:
time: 226 us; the launch traced here: 224 us
  Pallas kernels  215 us (95%)
  local copies, waits for them, and re-layouts  5 us (2%)
  other arithmetic  3.15 us (1%)
    pallas_call x1, Pallas kernels, products(): pl.pallas_call(functools.partial(exchange, (rows_axis, cols_axis), chunks...  180 us
    pallas_call x1, Pallas kernels, finish(): pl.pallas_call(functools.partial(finish_kernel, levels, count), out_shape...  35.2 us
    unnamed x13, local copies, waits for them, and re-layouts  5 us

profile of v4, /device:TPU:0, one launch (start us, length us, event | category | flops | bytes accessed | tf_op | source)
XLA Modules:
  0.0 223.8 jit_solution(2701855074962926901)
XLA Ops:
  0.6 0.0 copy-start
  0.7 0.7 copy-done
  1.3 0.1 broadcast_bitcast_fusion
  1.4 0.1 copy.10
  1.5 3.1 %select_bitcast_fusion.x_hbm = f32[2,512,512]{2,1,0:T(8,128)} fusion(f32[1,2,512,512]{3,2,1,0:T(8,128)} %param.6, pred[2,512]{1,0:T(4,128)(4,1)S(1)} %dynamic-slice_compare_fusion), kind=kLoop, calls=%fused_computation | loop fusion | flops 524288 | bytes 4195328 | tf_op jit(solution)/shard_map/squeeze | solution.py:394
  4.6 0.0 copy-start.2
  4.6 0.0 copy-start.3
  4.6 179.7 %shard_map.79 = (f32[2,512,512]{2,1,0:T(8,128)}, f32[2,512,512]{2,1,0:T(8,128)}) custom-call(f32[2048,2048]{1,0:T(8,128)} %a_hbm.1, f32[2,512,512]{2,1,0:T(8,128)} %select_bitcast_fusion.x_hbm), custom_call_target="tpu_custom_call" | custom-call | tf_op jit(solution)/shard_map/pallas_call | solution.py:235
  184.3 0.0 copy-done.2
  184.3 0.0 copy-done.3
  184.3 0.0 copy-start.1
  184.4 1.6 copy-done.1
  185.9 35.2 %shard_map.80 = (f32[2,512,512]{2,1,0:T(8,128)S(1)}, f32[2,128,128]{2,1,0:T(8,128)S(1)}, f32[128,128]{1,0:T(8,128)S(1)}) custom-call(f32[2,512,512]{2,1,0:T(8,128)S(1)} %copy-done.1, f32[2,512,512]{2,1,0:T(8,128)} %get-tuple-element.9.own_ref, f32[512,512]{1,0:T(8,128)S(1)} %bitcast.15, f32[2,128,128]{2,1,0:T(8,128)S(1)} %bitcast.17), custom_call_target="tpu_custom_call" | custom-call | tf_op jit(solution)/shard_map/pallas_call | solution.py:372
  221.1 1.3 copy.14
  222.5 0.7 copy.15
  223.1 0.6 copy.16
  (1 shorter events, 0.0 us)
Async XLA Ops:
  0.6 0.7 copy-start
  4.6 179.7 %copy-start.2 = (f32[1,512,512]{2,1,0:T(8,128)S(1)}, f32[1,512,512]{2,1,0:T(8,128)}, u32[]{:S(2)}) copy-start(f32[1,512,512]{2,1,0:T(8,128)} %param.7) | copy-start | bytes 3145732
  4.6 179.7 %copy-start.3 = (f32[1,2,128,128]{3,2,1,0:T(8,128)S(1)}, f32[1,2,128,128]{3,2,1,0:T(8,128)}, u32[]{:S(2)}) copy-start(f32[1,2,128,128]{3,2,1,0:T(8,128)} %param.8) | copy-start | bytes 393220
  184.3 1.6 copy-start.1
